TPU v7x, 32 devices: a whole 2x2x4 slice. The times are simulated.
32 devices in a mesh: groups: 2 (over y), row: 4 (over x, core), col: 4 (over z).
Axes of the slice: x: 2, y: 2, z: 4, core: 2. Of those that a mesh axis runs over, the one named last changes fastest.
Arguments:
- inputs: bfloat16 [1536, 4096], P(('groups', 'col'), 'row'), parts along dimension 0, may hold values from -6 to 6
- cotangent: bfloat16 [1536, 4096], P(('groups', 'col'), 'row'), parts along dimension 0, may hold values from -6 to 6
- preactivation: bfloat16 [1536, 8192], P(('groups', 'row'), 'col'), parts along dimension 0, may hold values from -8 to 8
- up_weight: bfloat16 [4096, 8192], P('row', 'col'), may hold values from -0.09375 to 0.09375
- down_weight: bfloat16 [8192, 4096], P('col', 'row'), may hold values from -0.0625 to 0.0625
Outputs:
- grad_input: bfloat16 [1536, 4096], P(('groups', 'col'), 'row'), parts along dimension 0
- grad_up: float32 [8192, 8192], P(('groups', 'row'), 'col'), parts along dimension 0
- grad_down: float32 [16384, 4096], P(('groups', 'col'), 'row'), parts along dimension 0
There are 2 independent parts, one for each index of `groups`. A program takes and returns all parts, laid end to end along the dimension named above; an argument that names none is the same for every part. Nothing has to cross between parts.
All inputs are finite; a program needn't handle non-finite values.
Results may differ from a plain program's by a relative error of at most 0.0049.
Values may be sent and summed in bfloat16 or wider, within the bound.
A program may use at most 128 MiB of HBM per device.

v0:
```python
import math
import jax
import jax.numpy as jnp
from jax import lax
from jax.sharding import PartitionSpec as P


def gelu_pair(values):
    v = values.astype(jnp.float32)
    tanh_arg = 0.7978845608 * (v + 0.044715 * v * v * v)
    tanh_val = jnp.tanh(tanh_arg)
    gelu_value = 0.5 * v * (1.0 + tanh_val)
    gelu_slope = 0.5 * (1.0 + tanh_val) + 0.5 * v * (1.0 - tanh_val * tanh_val) * 0.7978845608 * (
        1.0 + 3.0 * 0.044715 * v * v
    )
    return (gelu_value, gelu_slope)


def per_device(inputs, cotangent, preactivation, up_weight, down_weight):
    inputs_all, cotangent_all = (
        lax.all_gather(inputs, "col", axis=0, tiled=True),
        lax.all_gather(cotangent, "col", axis=0, tiled=True),
    )
    total_tokens = inputs_all.shape[0]
    token_scale = 1.0 / math.sqrt(total_tokens)
    last_dims = (((1,), (1,)), ((), ()))
    first_dims = (((0,), (0,)), ((), ()))
    piece = cotangent_all
    hidden_grad = lax.psum_scatter(
        lax.dot_general(piece, down_weight, last_dims, preferred_element_type=jnp.float32),
        "row",
        scatter_dimension=0,
        tiled=True,
    )
    gelu_value, gelu_slope = gelu_pair(preactivation)
    activation = gelu_value.astype(jnp.bfloat16)
    pre_grad = (hidden_grad * gelu_slope).astype(jnp.bfloat16)
    activation_all, pre_grad_all = (
        lax.all_gather(activation, "row", axis=0, tiled=True),
        lax.all_gather(pre_grad, "row", axis=0, tiled=True),
    )
    piece = pre_grad_all
    grad_input = lax.psum_scatter(
        lax.dot_general(piece, up_weight, last_dims, preferred_element_type=jnp.float32),
        "col",
        scatter_dimension=0,
        tiled=True,
    ).astype(jnp.bfloat16)
    grad_up = (
        lax.dot_general(inputs_all, pre_grad_all, first_dims, preferred_element_type=jnp.float32)
        * token_scale
    )
    grad_down = (
        lax.dot_general(
            activation_all, cotangent_all, first_dims, preferred_element_type=jnp.float32
        )
        * token_scale
    )
    return (grad_input, grad_up, grad_down)


def solution(mesh):
    placed = (
        P(("groups", "col"), "row"),
        P(("groups", "col"), "row"),
        P(("groups", "row"), "col"),
        P("row", "col"),
        P("col", "row"),
    )
    return jax.shard_map(
        per_device,
        mesh=mesh,
        in_specs=placed,
        out_specs=(
            P(("groups", "col"), "row"),
            P(("groups", "row"), "col"),
            P(("groups", "col"), "row"),
        ),
        check_vma=False,
    )
```

profile of v0, /device:TPU:0, one launch (start us, length us, event | category | flops | bytes accessed | tf_op | source)
XLA Modules:
  0.0 287.1 jit_solution(9059382792913873849)
XLA Ops:
  7.2 0.0 all-gather.5.cloned.1.call-start
  7.2 0.7 all-gather.5.cloned.1.call-update
  7.9 0.0 reduce-scatter.3.cloned.1.call-start
  7.9 41.4 %all-gather.5.cloned.1.call-done = bf16[768,1024]{1,0:T(8,128)(2,1)} async-done(((bf16[192,1024]{1,0:T(8,128)(2,1)}), bf16[768,1024]{1,0:T(8,128)(2,1)}) %all-gather.5.cloned.1.call-update) | async-done | bytes 1572880 | tf_op jit(solution)/shard_map/all_gather | solution.py:22
  49.3 8.8 %fusion.11 = f32[768,2048]{1,0:T(8,128)} fusion(bf16[768,1024]{1,0:T(8,128)(2,1)} %all-gather.5.cloned.1.call-done, bf16[2048,1024]{1,0:T(8,128)(2,1)} %param.9), kind=kOutput, calls=%fused_computation.20 | convolution fusion | flops 3221225472 | bytes 12058624 | tf_op jit(solution)/shard_map/dot_general | solution.py:30
  58.1 0.0 reduce-scatter.3.cloned.1.call-update
  58.2 0.0 all-gather.7.cloned.1.call-start
  58.2 57.8 %reduce-scatter.3.cloned.1.call-done = f32[192,2048]{1,0:T(8,128)} async-done(((f32[768,2048]{1,0:T(8,128)}), f32[192,2048]{1,0:T(8,128)}) %reduce-scatter.3.cloned.1.call-update) | async-done | bytes 1572880 | tf_op jit(solution)/shard_map/reduce_scatter | solution.py:29
  116.0 3.7 %fusion.7 = (bf16[192,2048]{1,0:T(8,128)(2,1)}, bf16[192,2048]{1,0:T(8,128)(2,1)}) fusion(bf16[192,2048]{1,0:T(8,128)(2,1)S(1)} %copy-done, f32[192,2048]{1,0:T(8,128)} %reduce-scatter.3.cloned.1.call-done), kind=kLoop, calls=%fused_computation.16 | loop fusion | flops 8650752 | bytes 3932160 | tf_op jit(solution)/shard_map/convert_element_type | solution.py:36
  119.7 0.0 all-gather.7.cloned.1.call-update
  119.7 0.0 all-gather.9.cloned.1.call-start
  119.8 0.5 all-gather.9.cloned.1.call-update
  120.3 0.0 all-gather.11.cloned.1.call-start
  120.4 0.5 all-gather.11.cloned.1.call-update
  120.9 0.0 reduce-scatter.5.cloned.1.call-start
  121.0 27.4 %all-gather.7.cloned.1.call-done = bf16[768,2048]{1,0:T(8,128)(2,1)} async-done(((bf16[192,2048]{1,0:T(8,128)(2,1)}), bf16[768,2048]{1,0:T(8,128)(2,1)}) %all-gather.7.cloned.1.call-update) | async-done | bytes 3145744 | tf_op jit(solution)/shard_map/all_gather | solution.py:40
  148.4 8.3 %fusion.12 = f32[768,1024]{1,0:T(8,128)} fusion(bf16[768,2048]{1,0:T(8,128)(2,1)} %all-gather.7.cloned.1.call-done, bf16[1024,2048]{1,0:T(8,128)(2,1)} %param.8), kind=kOutput, calls=%fused_computation.21 | convolution fusion | flops 3221225472 | bytes 10485760 | tf_op jit(solution)/shard_map/dot_general | solution.py:44
  156.7 30.2 %all-gather.9.cloned.1.call-done = bf16[768,1024]{1,0:T(8,128)(2,1)} async-done(((bf16[192,1024]{1,0:T(8,128)(2,1)}), bf16[768,1024]{1,0:T(8,128)(2,1)}) %all-gather.9.cloned.1.call-update) | async-done | bytes 1572880 | tf_op jit(solution)/shard_map/all_gather | solution.py:21
  186.9 7.1 %multiply_bitcast_fusion = f32[1024,2048]{0,1:T(8,128)} fusion(bf16[768,2048]{1,0:T(8,128)(2,1)S(1)} %copy-done.1, bf16[768,1024]{1,0:T(8,128)(2,1)} %all-gather.9.cloned.1.call-done), kind=kOutput, calls=%fused_computation | convolution fusion | flops 3223322624 | bytes 13107200 | tf_op jit(solution)/shard_map/dot_general | solution.py:50
  194.0 9.4 %copy.8 = f32[1024,2048]{1,0:T(8,128)} copy(f32[1024,2048]{0,1:T(8,128)} %multiply_bitcast_fusion) | data formatting | bytes 16777216
  203.4 12.3 %all-gather.11.cloned.1.call-done = bf16[768,2048]{1,0:T(8,128)(2,1)} async-done(((bf16[192,2048]{1,0:T(8,128)(2,1)}), bf16[768,2048]{1,0:T(8,128)(2,1)}) %all-gather.11.cloned.1.call-update) | async-done | bytes 3145744 | tf_op jit(solution)/shard_map/all_gather | solution.py:39
  215.7 7.6 %convolution_multiply_fusion = f32[2048,1024]{1,0:T(8,128)} fusion(bf16[768,2048]{1,0:T(8,128)(2,1)} %all-gather.11.cloned.1.call-done, bf16[768,1024]{1,0:T(8,128)(2,1)S(1)} %copy-done.2), kind=kOutput, calls=%fused_computation.1 | convolution fusion | flops 3223322624 | bytes 13107200 | tf_op jit(solution)/shard_map/dot_general | solution.py:54
  223.3 55.0 %reduce-scatter.5.cloned.1.call-done = f32[192,1024]{1,0:T(8,128)} async-done(((f32[768,1024]{1,0:T(8,128)}), f32[192,1024]{1,0:T(8,128)}) %reduce-scatter.5.cloned.1.call-update) | async-done | bytes 786448 | tf_op jit(solution)/shard_map/reduce_scatter | solution.py:43
  278.3 1.9 convert_element_type.14
  (7 shorter events, 0.0 us)
Async XLA Ops:
  7.2 42.2 %all-gather.5.cloned.1.call-start = ((), (), s32[]{:S(2)}) async-start(), calls=%async_computation.2 | async-start | bytes 1966080 | tf_op jit(solution)/shard_map/all_gather | solution.py:22
  7.9 108.1 %reduce-scatter.3.cloned.1.call-start = ((), (), s32[]{:S(2)}) async-start(), calls=%async_computation.3 | async-start | bytes 7864320 | tf_op jit(solution)/shard_map/reduce_scatter | solution.py:29
  58.1 57.9 %copy-start = (bf16[192,2048]{1,0:T(8,128)(2,1)S(1)}, bf16[192,2048]{1,0:T(8,128)(2,1)}, u32[]{:S(2)}) copy-start(bf16[192,2048]{1,0:T(8,128)(2,1)} %param.7) | copy-start | bytes 2359300
  58.2 90.2 %all-gather.7.cloned.1.call-start = ((), (), s32[]{:S(2)}) async-start(), calls=%async_computation.4 | async-start | bytes 3932160 | tf_op jit(solution)/shard_map/all_gather | solution.py:40
  119.7 67.1 %all-gather.9.cloned.1.call-start = ((), (), s32[]{:S(2)}) async-start(), calls=%async_computation.6 | async-start | bytes 1966080 | tf_op jit(solution)/shard_map/all_gather | solution.py:21
  120.3 95.4 %all-gather.11.cloned.1.call-start = ((), (), s32[]{:S(2)}) async-start(), calls=%async_computation.7 | async-start | bytes 3932160 | tf_op jit(solution)/shard_map/all_gather | solution.py:39
  120.9 157.4 %reduce-scatter.5.cloned.1.call-start = ((), (), s32[]{:S(2)}) async-start(), calls=%async_computation.5 | async-start | bytes 3932160 | tf_op jit(solution)/shard_map/reduce_scatter | solution.py:43
  156.7 30.2 %copy-start.1 = (bf16[768,2048]{1,0:T(8,128)(2,1)S(1)}, bf16[768,2048]{1,0:T(8,128)(2,1)}, u32[]{:S(2)}) copy-start(bf16[768,2048]{1,0:T(8,128)(2,1)} %all-gather.7.cloned.1.call-done) | copy-start | bytes 9437188
  194.0 21.7 %copy-start.2 = (bf16[768,1024]{1,0:T(8,128)(2,1)S(1)}, bf16[768,1024]{1,0:T(8,128)(2,1)}, u32[]{:S(2)}) copy-start(bf16[768,1024]{1,0:T(8,128)(2,1)} %all-gather.5.cloned.1.call-done) | copy-start | bytes 4718596
Sparse Core Ops, SparseCore 0:
  9.5 39.7 all-gather.4
  58.3 57.7 reduce-scatter.2
  119.9 28.4 all-gather.6
  149.8 37.0 all-gather.8
  188.3 27.3 all-gather.10
  217.9 60.3 reduce-scatter.4
where the time goes:
time: 287 us
  waiting for transfers between devices  226 us (79%)
  matrix products  31.8 us (11%)
  between operations  14.1 us (5%)
  local copies, waits for them, and re-layouts  9.45 us (3%)
  other arithmetic  5.61 us (2%)
    reduce_scatter x1, waiting for transfers between devices, per_device(): lax.psum_scatter(lax.dot_general(piece, down_weight, last_dims, preferred...  57.8 us
    reduce_scatter x1, waiting for transfers between devices, per_device(): lax.psum_scatter(lax.dot_general(piece, up_weight, last_dims, preferred_e...  55 us
    all_gather x1, waiting for transfers between devices, per_device(): lax.all_gather(cotangent, 'col', axis=0, tiled=True)  41.4 us
    all_gather x1, waiting for transfers between devices, per_device(): lax.all_gather(inputs, 'col', axis=0, tiled=True)  30.2 us
    all_gather x1, waiting for transfers between devices, per_device(): lax.all_gather(pre_grad, 'row', axis=0, tiled=True)  27.4 us
    all_gather x1, waiting for transfers between devices, per_device(): lax.all_gather(activation, 'row', axis=0, tiled=True)  12.3 us
    unnamed x7, local copies, waits for them, and re-layouts  9.45 us
    dot_general x1, matrix products, per_device(): lax.dot_general(piece, down_weight, last_dims, preferred_element_type=jnp...  8.82 us
  transfers between devices with their start and end apart: 6, of which 6 were waited for; matrix products, arithmetic and copies ran while one was open for 11% of the time, Pallas kernels for 0%

commit v1 on v0

--- a/solution.py
+++ b/solution.py
@@ -37,7 +37,9 @@
     pre_grad = (hidden_grad * gelu_slope).astype(jnp.bfloat16)
     activation_all, pre_grad_all = (
         lax.all_gather(activation, "row", axis=0, tiled=True),
-        lax.all_gather(pre_grad, "row", axis=0, tiled=True),
+        jnp.concatenate(
+            lax.all_to_all(jnp.stack([pre_grad] * lax.axis_size("row")), "row", 0, 0), axis=0
+        ),
     )
     piece = pre_grad_all
     grad_input = lax.psum_scatter(

time: 287 us -> 255 us (0.89)
  waiting for transfers between devices: 226 us -> 157 us
  blocking collectives: 0 us -> 39.7 us
  matrix products: 31.8 us -> 28.8 us
    all_to_all x0 -> x1, blocking collectives: none -> 39.7 us  [per_device(): lax.all_to_all(jnp.stack([pre_grad] * lax.axis_size('row')), 'row', 0, 0)]
    all_gather x1, waiting for transfers between devices: 30.2 us -> 0.02 us  [per_device(): lax.all_gather(inputs, 'col', axis=0, tiled=True)]
    all_gather x1 -> x0, waiting for transfers between devices: 27.4 us -> none  [per_device(): lax.all_gather(pre_grad, 'row', axis=0, tiled=True)]
    all_gather x1, waiting for transfers between devices: 12.3 us -> 2.18 us  [per_device(): lax.all_gather(activation, 'row', axis=0, tiled=True)]
    dot_general x1, matrix products: 8.27 us -> 5.23 us  [per_device(): lax.dot_general(piece, up_weight, last_dims, preferred_element_type=jnp.f...]
  transfers between devices with their start and end apart: 6 -> 5, of which waited for: 6 -> 4; matrix products, arithmetic and copies ran while one was open for 11% -> 13% of each run, Pallas kernels for 0% -> 0%
where the time goes in v1:
time: 255 us
  waiting for transfers between devices  157 us (62%)
  blocking collectives  39.7 us (16%)
  matrix products  28.8 us (11%)
  between operations  13.8 us (5%)
  local copies, waits for them, and re-layouts  9.66 us (4%)
  other arithmetic  5.36 us (2%)
    reduce_scatter x1, waiting for transfers between devices, per_device(): lax.psum_scatter(lax.dot_general(piece, down_weight, last_dims, preferred...  57.1 us
    reduce_scatter x1, waiting for transfers between devices, per_device(): lax.psum_scatter(lax.dot_general(piece, up_weight, last_dims, preferred_e...  55 us
    all_gather x1, waiting for transfers between devices, per_device(): lax.all_gather(cotangent, 'col', axis=0, tiled=True)  41.4 us
    all_to_all x1, blocking collectives, per_device(): lax.all_to_all(jnp.stack([pre_grad] * lax.axis_size('row')), 'row', 0, 0)  39.7 us
    unnamed x7, local copies, waits for them, and re-layouts  9.28 us
    dot_general x1, matrix products, per_device(): lax.dot_general(piece, down_weight, last_dims, preferred_element_type=jnp...  8.82 us
    dot_general x1, matrix products, per_device(): lax.dot_general(activation_all, cotangent_all, first_dims, preferred_elem...  7.6 us
    dot_general x1, matrix products, per_device(): lax.dot_general(inputs_all, pre_grad_all, first_dims, preferred_element_t...  7.13 us
  transfers between devices with their start and end apart: 5, of which 4 were waited for; matrix products, arithmetic and copies ran while one was open for 13% of the time, Pallas kernels for 0%

profile of v1, /device:TPU:0, one launch (start us, length us, event | category | flops | bytes accessed | tf_op | source)
XLA Modules:
  0.0 254.5 jit_solution(523620881591013865)
XLA Ops:
  7.2 0.0 all-gather.4.cloned.1.call-start
  7.2 0.7 all-gather.4.cloned.1.call-update
  7.9 0.0 reduce-scatter.3.cloned.1.call-start
  7.9 41.4 %all-gather.4.cloned.1.call-done = bf16[768,1024]{1,0:T(8,128)(2,1)} async-done(((bf16[192,1024]{1,0:T(8,128)(2,1)}), bf16[768,1024]{1,0:T(8,128)(2,1)}) %all-gather.4.cloned.1.call-update) | async-done | bytes 1572880 | tf_op jit(solution)/shard_map/all_gather | solution.py:22
  49.3 8.8 %fusion.11 = f32[768,2048]{1,0:T(8,128)} fusion(bf16[768,1024]{1,0:T(8,128)(2,1)} %all-gather.4.cloned.1.call-done, bf16[2048,1024]{1,0:T(8,128)(2,1)} %param.9), kind=kOutput, calls=%fused_computation.20 | convolution fusion | flops 3221225472 | bytes 12058624 | tf_op jit(solution)/shard_map/dot_general | solution.py:30
  58.1 0.0 reduce-scatter.3.cloned.1.call-update
  58.2 0.0 all-gather.6.cloned.1.call-start
  58.2 0.7 all-gather.6.cloned.1.call-update
  58.9 0.0 all-gather.8.cloned.1.call-start
  59.0 57.1 %reduce-scatter.3.cloned.1.call-done = f32[192,2048]{1,0:T(8,128)} async-done(((f32[768,2048]{1,0:T(8,128)}), f32[192,2048]{1,0:T(8,128)}) %reduce-scatter.3.cloned.1.call-update) | async-done | bytes 1572880 | tf_op jit(solution)/shard_map/reduce_scatter | solution.py:29
  116.0 3.4 %fusion.7 = (bf16[192,2048]{1,0:T(8,128)(2,1)}, bf16[192,2048]{1,0:T(8,128)(2,1)S(1)}) fusion(bf16[192,2048]{1,0:T(8,128)(2,1)S(1)} %copy-done, f32[192,2048]{1,0:T(8,128)} %reduce-scatter.3.cloned.1.call-done), kind=kLoop, calls=%fused_computation.16 | loop fusion | flops 8650752 | bytes 3932160 | tf_op jit(solution)/shard_map/convert_element_type | solution.py:36
  119.5 0.0 all-gather.8.cloned.1.call-update
  119.5 0.0 reduce-scatter.5.cloned.1.call-start
  119.5 0.4 stack.2
  119.9 39.7 %all_to_all.5 = bf16[4,192,2048]{2,1,0:T(8,128)(2,1)S(1)} all-to-all(bf16[4,192,2048]{2,1,0:T(8,128)(2,1)S(1)} %stack.2), channel_id=1, replica_groups=mesh['groups'=2,'row'=4,'col'=4] {'row'}, dimensions={0} | all-to-all | bytes 6291456 | tf_op jit(solution)/shard_map/all_to_all | solution.py:41
  159.6 5.2 %fusion.12 = f32[768,1024]{1,0:T(8,128)} fusion(bf16[768,2048]{1,0:T(8,128)(2,1)S(1)} %bitcast.11, bf16[1024,2048]{1,0:T(8,128)(2,1)S(1)} %copy-done.1), kind=kOutput, calls=%fused_computation.21 | convolution fusion | flops 3221225472 | bytes 10485760 | tf_op jit(solution)/shard_map/dot_general | solution.py:46
  164.9 0.0 reduce-scatter.5.cloned.1.call-update
  164.9 0.0 all-gather.6.cloned.1.call-done
  164.9 7.1 %multiply_bitcast_fusion = f32[1024,2048]{0,1:T(8,128)} fusion(bf16[768,2048]{1,0:T(8,128)(2,1)S(1)} %bitcast.12, bf16[768,1024]{1,0:T(8,128)(2,1)} %all-gather.6.cloned.1.call-done), kind=kOutput, calls=%fused_computation | convolution fusion | flops 3223322624 | bytes 13107200 | tf_op jit(solution)/shard_map/dot_general | solution.py:52
  172.0 9.3 %copy.8 = f32[1024,2048]{1,0:T(8,128)} copy(f32[1024,2048]{0,1:T(8,128)} %multiply_bitcast_fusion) | data formatting | bytes 16777216
  181.3 2.2 all-gather.8.cloned.1.call-done
  183.5 7.6 %convolution_multiply_fusion = f32[2048,1024]{1,0:T(8,128)} fusion(bf16[768,2048]{1,0:T(8,128)(2,1)} %all-gather.8.cloned.1.call-done, bf16[768,1024]{1,0:T(8,128)(2,1)S(1)} %copy-done.2), kind=kOutput, calls=%fused_computation.1 | convolution fusion | flops 3223322624 | bytes 13107200 | tf_op jit(solution)/shard_map/dot_general | solution.py:56
  191.1 55.0 %reduce-scatter.5.cloned.1.call-done = f32[192,1024]{1,0:T(8,128)} async-done(((f32[768,1024]{1,0:T(8,128)}), f32[192,1024]{1,0:T(8,128)}) %reduce-scatter.5.cloned.1.call-update) | async-done | bytes 786448 | tf_op jit(solution)/shard_map/reduce_scatter | solution.py:45
  246.1 1.9 convert_element_type.14
  (6 shorter events, 0.0 us)
Async XLA Ops:
  7.2 42.2 %all-gather.4.cloned.1.call-start = ((), (), s32[]{:S(2)}) async-start(), calls=%async_computation.3 | async-start | bytes 1966080 | tf_op jit(solution)/shard_map/all_gather | solution.py:22
  7.9 108.1 %reduce-scatter.3.cloned.1.call-start = ((), (), s32[]{:S(2)}) async-start(), calls=%async_computation.4 | async-start | bytes 7864320 | tf_op jit(solution)/shard_map/reduce_scatter | solution.py:29
  58.1 57.9 %copy-start = (bf16[192,2048]{1,0:T(8,128)(2,1)S(1)}, bf16[192,2048]{1,0:T(8,128)(2,1)}, u32[]{:S(2)}) copy-start(bf16[192,2048]{1,0:T(8,128)(2,1)} %param.7) | copy-start | bytes 2359300
  58.2 106.7 %all-gather.6.cloned.1.call-start = ((), (), s32[]{:S(2)}) async-start(), calls=%async_computation.6 | async-start | bytes 1966080 | tf_op jit(solution)/shard_map/all_gather | solution.py:21
  58.9 124.6 %all-gather.8.cloned.1.call-start = ((), (), s32[]{:S(2)}) async-start(), calls=%async_computation.7 | async-start | bytes 3932160 | tf_op jit(solution)/shard_map/all_gather | solution.py:39
  119.5 126.6 %reduce-scatter.5.cloned.1.call-start = ((), (), s32[]{:S(2)}) async-start(), calls=%async_computation.5 | async-start | bytes 3932160 | tf_op jit(solution)/shard_map/reduce_scatter | solution.py:45
  119.9 39.7 %copy-start.1 = (bf16[1024,2048]{1,0:T(8,128)(2,1)S(1)}, bf16[1024,2048]{1,0:T(8,128)(2,1)}, u32[]{:S(2)}) copy-start(bf16[1024,2048]{1,0:T(8,128)(2,1)} %param.8) | copy-start | bytes 12582916
  172.0 11.5 %copy-start.2 = (bf16[768,1024]{1,0:T(8,128)(2,1)S(1)}, bf16[768,1024]{1,0:T(8,128)(2,1)}, u32[]{:S(2)}) copy-start(bf16[768,1024]{1,0:T(8,128)(2,1)} %all-gather.4.cloned.1.call-done) | copy-start | bytes 4718596
Sparse Core Ops, SparseCore 0:
  9.5 39.7 all-gather.3
  58.3 57.7 reduce-scatter.2
  117.6 37.0 all-gather.5
  156.1 27.3 all-gather.7
  185.6 60.3 reduce-scatter.4
